TPU v7x, 32 devices: a whole 2x2x4 slice. The times are simulated.
32 devices in a mesh: dp: 8 (over y, x, core), tensor: 4 (over z).
Axes of the slice: x: 2, y: 2, z: 4, core: 2. Of those that a mesh axis runs over, the one named last changes fastest.
Arguments:
- tokens: bfloat16 [18432, 768], P(('dp', 'tensor')), may hold values from -6 to 6
- segment_ids: int32 [8, 2304], P('dp'), may hold values from 0 to 7, never falling along the last dimension, each value on 1 to 1152 neighbouring positions
- ln1_gain: float32 [768], replicated, may hold values from 0.5 to 1.5
- ln1_bias: float32 [768], replicated, may hold values from -3 to 3
- qkv_weight: bfloat16 [3, 768, 768], P(None, None, 'tensor'), may hold values from -0.21875 to 0.21875
- qv_bias: float32 [2, 768], P(None, 'tensor'), may hold values from -3 to 3
- proj_weight: bfloat16 [768, 768], P('tensor'), may hold values from -0.875 to 0.875
- proj_bias: float32 [768], replicated, may hold values from -1.75 to 1.75
- scale_one: float32 [768], replicated, may hold values from 0.3 to 1.5
- ln2_gain: float32 [768], replicated, may hold values from 0.5 to 1.5
- ln2_bias: float32 [768], replicated, may hold values from -3 to 3
- fc1_weight: bfloat16 [768, 3072], P(None, 'tensor'), may hold values from -0.21875 to 0.21875
- fc1_bias: float32 [3072], P('tensor'), may hold values from -3 to 3
- fc2_weight: bfloat16 [3072, 768], P('tensor'), may hold values from -0.15625 to 0.15625
- fc2_bias: float32 [768], replicated, may hold values from -1.75 to 1.75
- scale_two: float32 [768], replicated, may hold values from 0.3 to 1.5
- cotangent: bfloat16 [18432, 768], P(('dp', 'tensor')), may hold values from -6 to 6
Outputs:
- block_out: bfloat16 [18432, 768], P(('dp', 'tensor'))
- grad_tokens: float32 [18432, 768], P(('dp', 'tensor'))
- grad_ln1_gain: float32 [768], replicated
- grad_ln1_bias: float32 [768], replicated
- grad_qkv_weight: float32 [3, 768, 768], P(None, None, 'tensor')
- grad_qv_bias: float32 [2, 768], P(None, 'tensor')
- grad_proj_weight: float32 [768, 768], P('tensor')
- grad_proj_bias: float32 [768], replicated
- grad_scale_one: float32 [768], replicated
- grad_ln2_gain: float32 [768], replicated
- grad_ln2_bias: float32 [768], replicated
- grad_fc1_weight: float32 [768, 3072], P(None, 'tensor')
- grad_fc1_bias: float32 [3072], P('tensor')
- grad_fc2_weight: float32 [3072, 768], P('tensor')
- grad_fc2_bias: float32 [768], replicated
- grad_scale_two: float32 [768], replicated
Inputs may be any that keep to these rules, and one draw needn't show every extreme that they name: `segment_ids`: within a sequence the ids never fall; every segment holds at most 1152 tokens, and some segment holds exactly 1152.
All inputs are finite; a program needn't handle non-finite values.
Results may differ from a plain program's by a relative error of at most 0.015.
Values may be sent and summed in bfloat16 or wider, within the bound.
A program may use at most 128 MiB of HBM per device.

v0:
```python
from functools import partial
import jax
import jax.numpy as jnp
from jax import lax
from jax.sharding import PartitionSpec as P

HEAD_DIM = 64
eps_norm = 1e-06


def normalize(rows_in, gain, shift):
    row_mean = jnp.mean(rows_in, axis=1, keepdims=True)
    centred = rows_in - row_mean
    inverse = lax.rsqrt(jnp.mean(centred * centred, axis=1, keepdims=True) + eps_norm)
    unit_rows = centred * inverse
    return (unit_rows * gain + shift, unit_rows, inverse)


def normalize_back(grad_rows, unit_rows, inverse, gain):
    scaled = grad_rows * gain
    inner = (
        scaled
        - jnp.mean(scaled, axis=1, keepdims=True)
        - unit_rows * jnp.mean(scaled * unit_rows, axis=1, keepdims=True)
    )
    return (inverse * inner, jnp.sum(grad_rows * unit_rows, axis=0), jnp.sum(grad_rows, axis=0))


def sum_mlp(first_grad, second_grad, third_grad):
    return lax.psum((first_grad, second_grad, third_grad), "dp")


def on_device(
    tokens,
    segment_ids,
    ln1_gain,
    ln1_bias,
    qkv_weight,
    qv_bias,
    proj_weight,
    proj_bias,
    scale_one,
    ln2_gain,
    ln2_bias,
    fc1_weight,
    fc1_bias,
    fc2_weight,
    fc2_bias,
    scale_two,
    cotangent,
):
    seq_len = segment_ids.shape[1]
    heads_here = qkv_weight.shape[2] // HEAD_DIM
    image_ids = segment_ids[0]
    score_scale = HEAD_DIM ** (-0.5)
    block_rows = 576
    block_count = seq_len // block_rows
    starts = jnp.arange(block_count, dtype=jnp.int32) * block_rows
    inputs = tokens.astype(jnp.float32)
    normed1, unit_one, inverse_one = normalize(inputs, ln1_gain, ln1_bias)
    full_one = lax.all_gather(normed1.astype(jnp.bfloat16), "tensor", axis=0, tiled=True)
    projected = jnp.einsum("sd,tde->tse", full_one, qkv_weight, preferred_element_type=jnp.float32)
    queries = (
        (projected[0] + qv_bias[0]).astype(jnp.bfloat16).reshape(seq_len, heads_here, HEAD_DIM)
    )
    key_rows = projected[1].astype(jnp.bfloat16).reshape(seq_len, heads_here, HEAD_DIM)
    value_rows = (
        (projected[2] + qv_bias[1]).astype(jnp.bfloat16).reshape(seq_len, heads_here, HEAD_DIM)
    )

    def scores_of(first_row):
        query_block = lax.dynamic_slice_in_dim(queries, first_row, block_rows, 0)
        id_block = lax.dynamic_slice_in_dim(image_ids, first_row, block_rows, 0)
        raw_scores = (
            jnp.einsum("qhd,khd->hqk", query_block, key_rows, preferred_element_type=jnp.float32)
            * score_scale
        )
        same_image = id_block[:, None] == image_ids[None, :]
        return (jnp.where(same_image[None], raw_scores, -1e30), query_block)

    def forward_block(first_row):
        scores, query_block = scores_of(first_row)
        row_peak = jnp.max(scores, axis=-1, keepdims=True)
        weights = jnp.exp(scores - row_peak)
        row_total = jnp.sum(weights, axis=-1, keepdims=True)
        softmax = (weights / row_total).astype(jnp.bfloat16)
        mixture = jnp.einsum(
            "hqk,khd->qhd", softmax, value_rows, preferred_element_type=jnp.float32
        )
        return (mixture.astype(jnp.bfloat16), (row_peak + jnp.log(row_total))[..., 0])

    mixtures, log_totals = lax.map(forward_block, starts)
    attended = mixtures.reshape(seq_len, heads_here * HEAD_DIM)
    branch = (
        lax.psum_scatter(
            jnp.dot(attended, proj_weight, preferred_element_type=jnp.float32),
            "tensor",
            scatter_dimension=0,
            tiled=True,
        )
        + proj_bias
    )
    hidden = inputs + scale_one * branch
    normed2, unit_two, inverse_two = normalize(hidden, ln2_gain, ln2_bias)
    full_two = lax.all_gather(normed2.astype(jnp.bfloat16), "tensor", axis=0, tiled=True)
    pre_act = jnp.dot(full_two, fc1_weight, preferred_element_type=jnp.float32) + fc1_bias
    active = jax.nn.gelu(pre_act, approximate=False).astype(jnp.bfloat16)
    mlp_out = (
        lax.psum_scatter(
            jnp.dot(active, fc2_weight, preferred_element_type=jnp.float32).astype(jnp.bfloat16),
            "tensor",
            scatter_dimension=0,
            tiled=True,
        ).astype(jnp.float32)
        + fc2_bias
    )
    block_out = (hidden + scale_two * mlp_out).astype(jnp.bfloat16)
    grad_out = cotangent.astype(jnp.float32)
    grad_scale_two = jnp.sum(grad_out * mlp_out, axis=0)
    grad_mlp = (grad_out * scale_two).astype(jnp.bfloat16)
    grad_fc2_bias = jnp.sum(grad_mlp.astype(jnp.float32), axis=0)
    grad_mlp_full = lax.all_gather(grad_mlp, "tensor", axis=0, tiled=True)
    grad_fc2_weight = jnp.einsum(
        "sf,sd->fd", active, grad_mlp_full, preferred_element_type=jnp.float32
    )
    grad_active = jnp.einsum(
        "sd,fd->sf", grad_mlp_full, fc2_weight, preferred_element_type=jnp.float32
    )
    gelu_value, gelu_back = jax.vjp(partial(jax.nn.gelu, approximate=False), pre_act)
    grad_pre = gelu_back(grad_active)[0].astype(jnp.bfloat16)
    grad_fc1_bias = jnp.sum(grad_pre.astype(jnp.float32), axis=0)
    grad_fc1_weight = jnp.einsum(
        "sd,sf->df", full_two, grad_pre, preferred_element_type=jnp.float32
    )
    grad_normed2 = lax.psum_scatter(
        jnp.einsum("sf,df->sd", grad_pre, fc1_weight, preferred_element_type=jnp.float32),
        "tensor",
        scatter_dimension=0,
        tiled=True,
    )
    grad_ln2_in, grad_ln2_gain, grad_ln2_bias = normalize_back(
        grad_normed2, unit_two, inverse_two, ln2_gain
    )
    grad_hidden = grad_out + grad_ln2_in
    grad_scale_one = jnp.sum(grad_hidden * branch, axis=0)
    grad_branch = (grad_hidden * scale_one).astype(jnp.bfloat16)
    grad_proj_bias = jnp.sum(grad_branch.astype(jnp.float32), axis=0)
    grad_branch_full = lax.all_gather(grad_branch, "tensor", axis=0, tiled=True)
    grad_proj_weight = jnp.einsum(
        "se,sd->ed", attended, grad_branch_full, preferred_element_type=jnp.float32
    )
    grad_attended = jnp.einsum(
        "sd,ed->se", grad_branch_full, proj_weight, preferred_element_type=jnp.float32
    )
    grad_heads = grad_attended.astype(jnp.bfloat16).reshape(seq_len, heads_here, HEAD_DIM)

    def backward_block(running, block_item):
        first_row, log_total = block_item
        grad_keys, grad_values = running
        scores, query_block = scores_of(first_row)
        probs = jnp.exp(scores - log_total[..., None])
        grad_block = lax.dynamic_slice_in_dim(grad_heads, first_row, block_rows, 0)
        grad_probs = jnp.einsum(
            "qhd,khd->hqk", grad_block, value_rows, preferred_element_type=jnp.float32
        )
        grad_values = grad_values + jnp.einsum(
            "hqk,qhd->khd",
            probs.astype(jnp.bfloat16),
            grad_block,
            preferred_element_type=jnp.float32,
        )
        shared = jnp.sum(probs * grad_probs, axis=-1, keepdims=True)
        grad_scores = (probs * (grad_probs - shared)).astype(jnp.bfloat16)
        grad_query = (
            jnp.einsum("hqk,khd->qhd", grad_scores, key_rows, preferred_element_type=jnp.float32)
            * score_scale
        )
        grad_keys = (
            grad_keys
            + jnp.einsum(
                "hqk,qhd->khd", grad_scores, query_block, preferred_element_type=jnp.float32
            )
            * score_scale
        )
        return ((grad_keys, grad_values), grad_query)

    empty = jnp.zeros((seq_len, heads_here, HEAD_DIM), jnp.float32)
    (grad_keys, grad_values), grad_queries = lax.scan(
        backward_block, (empty, empty), (starts, log_totals)
    )
    columns = heads_here * HEAD_DIM
    grad_query_rows = grad_queries.reshape(seq_len, columns).astype(jnp.bfloat16)
    grad_key_rows = grad_keys.reshape(seq_len, columns).astype(jnp.bfloat16)
    grad_value_rows = grad_values.reshape(seq_len, columns).astype(jnp.bfloat16)
    stacked = jnp.stack([grad_query_rows, grad_key_rows, grad_value_rows])
    grad_qv_bias = jnp.stack(
        [
            jnp.sum(grad_query_rows.astype(jnp.float32), axis=0),
            jnp.sum(grad_value_rows.astype(jnp.float32), axis=0),
        ]
    )
    grad_qkv_weight = jnp.einsum(
        "sd,tse->tde", full_one, stacked, preferred_element_type=jnp.float32
    )
    grad_normed1 = lax.psum_scatter(
        jnp.einsum("tse,tde->sd", stacked, qkv_weight, preferred_element_type=jnp.float32).astype(
            jnp.bfloat16
        ),
        "tensor",
        scatter_dimension=0,
        tiled=True,
    ).astype(jnp.float32)
    grad_ln1_in, grad_ln1_gain, grad_ln1_bias = normalize_back(
        grad_normed1, unit_one, inverse_one, ln1_gain
    )
    grad_tokens = grad_hidden + grad_ln1_in
    grad_fc2_weight, grad_fc1_weight, grad_fc1_bias = sum_mlp(
        grad_fc2_weight, grad_fc1_weight, grad_fc1_bias
    )
    grad_qkv_weight, grad_qv_bias, grad_proj_weight = lax.psum(
        (grad_qkv_weight, grad_qv_bias, grad_proj_weight), "dp"
    )
    (
        grad_ln1_gain,
        grad_ln1_bias,
        grad_proj_bias,
        grad_scale_one,
        grad_ln2_gain,
        grad_ln2_bias,
        grad_fc2_bias,
        grad_scale_two,
    ) = lax.psum(
        (
            grad_ln1_gain,
            grad_ln1_bias,
            grad_proj_bias,
            grad_scale_one,
            grad_ln2_gain,
            grad_ln2_bias,
            grad_fc2_bias,
            grad_scale_two,
        ),
        ("dp", "tensor"),
    )
    return (
        block_out,
        grad_tokens,
        grad_ln1_gain,
        grad_ln1_bias,
        grad_qkv_weight,
        grad_qv_bias,
        grad_proj_weight,
        grad_proj_bias,
        grad_scale_one,
        grad_ln2_gain,
        grad_ln2_bias,
        grad_fc1_weight,
        grad_fc1_bias,
        grad_fc2_weight,
        grad_fc2_bias,
        grad_scale_two,
    )


def solution(mesh):
    return jax.shard_map(
        on_device,
        mesh=mesh,
        in_specs=(
            P(("dp", "tensor"), None),
            P("dp", None),
            P(),
            P(),
            P(None, None, "tensor"),
            P(None, "tensor"),
            P("tensor", None),
            P(),
            P(),
            P(),
            P(),
            P(None, "tensor"),
            P("tensor"),
            P("tensor", None),
            P(),
            P(),
            P(("dp", "tensor"), None),
        ),
        out_specs=(
            P(("dp", "tensor"), None),
            P(("dp", "tensor"), None),
            P(),
            P(),
            P(None, None, "tensor"),
            P(None, "tensor"),
            P("tensor", None),
            P(),
            P(),
            P(),
            P(),
            P(None, "tensor"),
            P("tensor"),
            P("tensor", None),
            P(),
            P(),
        ),
        check_vma=False,
    )
```

profile of v0, /device:TPU:0, one launch (start us, length us, event | category | flops | bytes accessed | tf_op | source)
XLA Modules:
  0.0 1202.9 jit_solution(1889019132003992440)
XLA Ops:
  13.2 72.5 %all-gather.5.cloned.1.call-done = bf16[2304,768]{1,0:T(8,128)(2,1)} async-done(((bf16[576,768]{1,0:T(8,128)(2,1)}), bf16[2304,768]{1,0:T(8,128)(2,1)}) %all-gather.5.cloned.1.call-update) | async-done | bytes 3538960 | tf_op jit(solution)/shard_map/all_gather | solution.py:61
  91.9 132.6 %while.27 = (s32[]{:T(128)}, bf16[4,576,3,64]{1,3,2,0:T(8,128)(2,1)}, f32[4,3,576]{2,1,0:T(4,128)S(1)}, s32[4]{0:T(128)S(1)}, s32[2304]{0:T(1024)S(1)}, /*index=...) while((s32[]{:T(128)}, ...), condition=%wide.region_5.6_spmd, body=%wide.region_2.5_spmd.sunk | while | flops 1068427584 | bytes 55445184 | solution.py:92
  103.9 10.0 fusion.122
  113.9 11.2 fusion.123
  137.0 10.0 fusion.122
  147.0 11.2 fusion.123
  180.1 11.2 fusion.123
  213.1 11.2 fusion.123
  233.7 122.2 %reduce-scatter.5.cloned.1.call-done = f32[576,768]{1,0:T(8,128)} async-done(((f32[2304,768]{1,0:T(8,128)}), f32[576,768]{1,0:T(8,128)}) %reduce-scatter.5.cloned.1.call-update) | async-done | bytes 1769488 | tf_op jit(solution)/shard_map/reduce_scatter | solution.py:95
  362.1 68.8 %all-gather.7.cloned.1.call-done = bf16[2304,768]{1,0:T(8,128)(2,1)} async-done(((bf16[576,768]{1,0:T(8,128)(2,1)}), bf16[2304,768]{1,0:T(8,128)(2,1)}) %all-gather.7.cloned.1.call-update) | async-done | bytes 3538960 | tf_op jit(solution)/shard_map/all_gather | solution.py:105
  439.2 62.4 %all-gather.9.cloned.1.call-done = bf16[2304,768]{1,0:T(8,128)(2,1)} async-done(((bf16[576,768]{1,0:T(8,128)(2,1)}), bf16[2304,768]{1,0:T(8,128)(2,1)}) %all-gather.9.cloned.1.call-update) | async-done | bytes 3538960 | tf_op jit(solution)/shard_map/all_gather | solution.py:122
  501.6 22.6 %convert_reduce_fusion = (f32[768]{0:T(1024)}, bf16[2304,768]{1,0:T(8,128)(2,1)S(1)}, f32[2304,768]{1,0:T(8,128)}) fusion(f32[2304,768]{1,0:T(8,128)} %fusion.68, f32[768]{0:T(1024)S(1)} %copy-done.47, bf16[2304,768]{1,0:T(8,128)(2,1)} %all-gather.9.cloned.1.call-done, bf16[768,768]{1,0:T(8,128)(2,1)S(1)} %copy-done), kind=kOutput, calls=%fused_computation.43 | convolution fusion | flops 2850618624 | bytes 22419456 | tf_op jit(solution)/shard_map/sd,fd->sf/dot_general | solution.py:126
  543.7 109.6 %reduce-scatter.9.cloned.1.call-done = f32[576,768]{1,0:T(8,128)} async-done(((f32[2304,768]{1,0:T(8,128)}), f32[576,768]{1,0:T(8,128)}) %reduce-scatter.9.cloned.1.call-update) | async-done | bytes 1769488 | tf_op jit(solution)/shard_map/reduce_scatter | solution.py:135
  656.7 65.7 %reduce-scatter.7.cloned.1.call-done = bf16[576,768]{1,0:T(8,128)(2,1)} async-done(((bf16[2304,768]{1,0:T(8,128)(2,1)}), bf16[576,768]{1,0:T(8,128)(2,1)}) %reduce-scatter.7.cloned.1.call-update) | async-done | bytes 884752 | tf_op jit(solution)/shard_map/reduce_scatter | solution.py:109
  730.2 70.3 %all-gather.11.cloned.1.call-done = bf16[2304,768]{1,0:T(8,128)(2,1)} async-done(((bf16[576,768]{1,0:T(8,128)(2,1)}), bf16[2304,768]{1,0:T(8,128)(2,1)}) %all-gather.11.cloned.1.call-update) | async-done | bytes 3538960 | tf_op jit(solution)/shard_map/all_gather | solution.py:148
  803.8 188.0 %while.28 = (s32[]{:T(128)}, f32[2304,3,64]{0,2,1:T(8,128)}, f32[2304,3,64]{0,2,1:T(8,128)}, bf16[4,576,3,64]{1,3,2,0:T(8,128)(2,1)}, s32[4]{0:T(128)S(1)}, /*in...) while((s32[]{:T(128)}, f32[2304,3,64]{0,2,1:T(8,128)}, ...), condition=%wide.region_15.16_spmd.clone, body=%wide.region_13.15_spmd.clone.sunk | while | flops 2587519232 | bytes 182914960 | solution.py:188
  816.6 10.3 multiply_reduce_fusion.7
  862.6 10.3 multiply_reduce_fusion.7
  909.8 10.3 multiply_reduce_fusion.7
  957.0 10.4 multiply_reduce_fusion.7
  1024.4 15.2 %all-reduce.1 = (f32[2,192]{1,0:T(2,128)}, f32[768]{0:T(1024)}) all-reduce(f32[2,192]{1,0:T(2,128)S(1)} %pad_maximum_fusion.3, f32[768]{0:T(1024)S(1)} %copy-done.49), channel_id=1, replica_groups=mesh['dp'=8,'tensor'=4] {'dp'}, use_global_device_ids=true, to_apply=%region_26.27 | all-reduce | flops 1152 | bytes 9216 | tf_op jit(solution)/shard_map/psum | solution.py:220
  1039.6 30.6 %reduce-scatter.11.cloned.1.call-done = bf16[576,768]{1,0:T(8,128)(2,1)} async-done(((bf16[2304,768]{1,0:T(8,128)(2,1)}), bf16[576,768]{1,0:T(8,128)(2,1)}) %reduce-scatter.11.cloned.1.call-update) | async-done | bytes 884752 | tf_op jit(solution)/shard_map/reduce_scatter | solution.py:205
  1072.4 42.2 %all-reduce = (f32[768]{0:T(1024)}, f32[768]{0:T(1024)}, f32[768]{0:T(1024)}, f32[768]{0:T(1024)}, f32[768]{0:T(1024)}, /*index=5*/f32[768]{0:T(1024)}, f32[768]{0:T(1024)}, f32[768]{0:T(1024)}) all-reduce(f32[768]{0:T(1024)S(1)} %get-tuple-element.174, ...), channel_id=1, replica_groups=mesh['dp'=8,'tensor'=4] {'dp','tensor'}, use_global_device_ids=true, to_apply=%region_20.21 | all-reduce | flops 6144 | bytes 49152 | tf_op jit(solution)/shard_map/psum | solution.py:232
  1117.6 72.0 %all-reduce.5.cloned.1.call-done = (f32[3,768,192]{1,2,0:T(8,128)}, f32[192,768]{1,0:T(8,128)}, f32[768,768]{1,0:T(8,128)}, f32[768,768]{1,0:T(8,128)}) async-done(((f32[3,768,192]{1,2,0:T(8,128)}, f32[192,768]{1,0:T(8,128)}, f32[768,768]{1,0:T(8,128)}, f32[768,768]{1,0:T(8,128)}), (f32[3,768,192]{1,2,0:T(8,128)}, f32[192,768]{1,0:T(8,128)}, f32[768,768]{1,0:T(8,128)}, ...) | async-done | bytes 7077904 | tf_op jit(solution)/shard_map/psum | solution.py:220
  (291 shorter events, 311.7 us)
Async XLA Ops:
  7.2 494.4 %copy-start = (bf16[768,768]{1,0:T(8,128)(2,1)S(1)}, bf16[768,768]{1,0:T(8,128)(2,1)}, u32[]{:S(2)}) copy-start(bf16[768,768]{1,0:T(8,128)(2,1)} %param.34) | copy-start | bytes 3538948
  7.2 78.5 %copy-start.54 = (bf16[3,768,192]{1,2,0:T(8,128)(2,1)S(1)}, bf16[3,768,192]{1,2,0:T(8,128)(2,1)}, u32[]{:S(2)}) copy-start(bf16[3,768,192]{1,2,0:T(8,128)(2,1)} %param.25) | copy-start | bytes 2654212
  7.2 78.5 %all-gather.5.cloned.1.call-start = ((), (), s32[]{:S(2)}) async-start(), calls=%async_computation.4 | async-start | bytes 4423680 | tf_op jit(solution)/shard_map/all_gather | solution.py:61
  8.8 81.2 %copy-start.31 = (f32[576]{0:T(1024)}, f32[576]{0:T(1024)S(1)}, u32[]{:S(2)}) copy-start(f32[576]{0:T(1024)S(1)} %broadcast_multiply_fusion.5) | copy-start | bytes 6916
  10.4 79.6 %copy-start.33 = (f32[576]{0:T(1024)}, f32[576]{0:T(1024)S(1)}, u32[]{:S(2)}) copy-start(f32[576]{0:T(1024)S(1)} %add_rsqrt_fusion.1) | copy-start | bytes 6916
  12.9 343.0 %reduce-scatter.5.cloned.1.call-start = ((), (), s32[]{:S(2)}) async-start(), calls=%async_computation.5 | async-start | bytes 8847360 | tf_op jit(solution)/shard_map/reduce_scatter | solution.py:95
  233.6 122.3 %copy-start.6 = (bf16[576,768]{1,0:T(8,128)(2,1)S(1)}, bf16[576,768]{1,0:T(8,128)(2,1)}, u32[]{:S(2)}) copy-start(bf16[576,768]{1,0:T(8,128)(2,1)} %param.21) | copy-start | bytes 2654212
  233.6 122.3 %copy-start.37 = (f32[768]{0:T(1024)S(1)}, f32[768]{0:T(1024)}, u32[]{:S(2)}) copy-start(f32[768]{0:T(1024)} %param.28) | copy-start | bytes 9220
  233.6 122.3 %copy-start.39 = (f32[768]{0:T(1024)S(1)}, f32[768]{0:T(1024)}, u32[]{:S(2)}) copy-start(f32[768]{0:T(1024)} %param.29) | copy-start | bytes 9220
  233.7 125.3 %copy-start.36 = (f32[768]{0:T(1024)S(1)}, f32[768]{0:T(1024)}, u32[]{:S(2)}) copy-start(f32[768]{0:T(1024)} %param.30) | copy-start | bytes 9220
  233.7 125.3 %copy-start.46 = (f32[768]{0:T(1024)S(1)}, f32[768]{0:T(1024)}, u32[]{:S(2)}) copy-start(f32[768]{0:T(1024)} %param.31) | copy-start | bytes 9220
  233.7 197.2 %all-gather.7.cloned.1.call-start = ((), (), s32[]{:S(2)}) async-start(), calls=%async_computation.6 | async-start | bytes 4423680 | tf_op jit(solution)/shard_map/all_gather | solution.py:105
  360.3 141.3 %all-gather.9.cloned.1.call-start = ((), (), s32[]{:S(2)}) async-start(), calls=%async_computation.8 | async-start | bytes 4423680 | tf_op jit(solution)/shard_map/all_gather | solution.py:122
  362.1 139.5 %copy-start.47 = (f32[768]{0:T(1024)S(1)}, f32[768]{0:T(1024)}, u32[]{:S(2)}) copy-start(f32[768]{0:T(1024)} %param.33) | copy-start | bytes 9220
  362.1 291.2 %reduce-scatter.9.cloned.1.call-start = ((), (), s32[]{:S(2)}) async-start(), calls=%async_computation.9 | async-start | bytes 8847360 | tf_op jit(solution)/shard_map/reduce_scatter | solution.py:135
  531.1 191.3 %reduce-scatter.7.cloned.1.call-start = ((), (), s32[]{:S(2)}) async-start(), calls=%async_computation.7 | async-start | bytes 4423680 | tf_op jit(solution)/shard_map/reduce_scatter | solution.py:109
  543.7 178.7 %copy-start.48 = (f32[768]{0:T(1024)S(1)}, f32[768]{0:T(1024)}, u32[]{:S(2)}) copy-start(f32[768]{0:T(1024)} %param.35) | copy-start | bytes 9220
  543.7 256.8 %all-gather.11.cloned.1.call-start = ((), (), s32[]{:S(2)}) async-start(), calls=%async_computation.10 | async-start | bytes 4423680 | tf_op jit(solution)/shard_map/all_gather | solution.py:148
  730.1 73.8 %copy-start.8 = (bf16[2304,3,64]{0,2,1:T(8,128)(2,1)S(1)}, bf16[2304,3,64]{0,2,1:T(8,128)(2,1)}, u32[]{:S(2)}) copy-start(bf16[2304,3,64]{0,2,1:T(8,128)(2,1)} %get-tuple-element.513) | copy-start | bytes 2654212
  730.1 340.1 %reduce-scatter.11.cloned.1.call-start = ((), (), s32[]{:S(2)}) async-start(), calls=%async_computation.11 | async-start | bytes 4423680 | tf_op jit(solution)/shard_map/reduce_scatter | solution.py:205
  1005.1 184.5 %all-reduce.5.cloned.1.call-start = ((), (), s32[]{:S(2)}) async-start(), calls=%async_computation.12 | async-start | bytes 14155776 | tf_op jit(solution)/shard_map/psum | solution.py:220
  1022.5 49.8 %copy-start.40 = (f32[768]{0:T(1024)S(1)}, f32[768]{0:T(1024)}, u32[]{:S(2)}) copy-start(f32[768]{0:T(1024)} %get-tuple-element.243) | copy-start | bytes 9220
  1022.5 49.8 %copy-start.41 = (f32[768]{0:T(1024)S(1)}, f32[768]{0:T(1024)}, u32[]{:S(2)}) copy-start(f32[768]{0:T(1024)} %get-tuple-element.245) | copy-start | bytes 9220
  1022.6 92.0 %copy-start.11 = (f32[576,768]{1,0:T(8,128)S(1)}, f32[576,768]{1,0:T(8,128)}, u32[]{:S(2)}) copy-start(f32[576,768]{1,0:T(8,128)} %copy-done.10) | copy-start | bytes 5308420
  (59 other events, 631.3 us)
Sparse Core Ops, SparseCore 0:
  13.0 72.6 all-gather.4
  233.8 122.0 reduce-scatter.4
  360.4 70.4 all-gather.6
  432.9 68.5 all-gather.8
  531.2 122.0 reduce-scatter.8
  655.5 66.8 reduce-scatter.6
  730.2 70.2 all-gather.10
  1005.2 64.9 reduce-scatter.10
  1075.1 114.4 all-reduce.4
where the time goes:
time: 1210 us; the launch traced here: 1200 us
  waiting for transfers between devices  674 us (56%)
  matrix products  286 us (24%)
  other arithmetic  126 us (10%)
  blocking collectives  57.3 us (5%)
  local copies, waits for them, and re-layouts  27.9 us (2%)
  loops' own time  16.4 us (1%)
  between operations  14.6 us (1%)
    reduce_scatter x1, waiting for transfers between devices, on_device(): lax.psum_scatter(jnp.dot(attended, proj_weight, preferred_element_type=jn...  122 us
    reduce_scatter x1, waiting for transfers between devices, on_device(): lax.psum_scatter(jnp.einsum('sf,df->sd', grad_pre, fc1_weight, preferred_...  110 us
    dot_general x8, matrix products, scores_of(): jnp.einsum('qhd,khd->hqk', query_block, key_rows, preferred_element_type=...  75.1 us
    all_gather x1, waiting for transfers between devices, on_device(): lax.all_gather(normed1.astype(jnp.bfloat16), 'tensor', axis=0, tiled=True)  72.5 us
    psum x1, waiting for transfers between devices, on_device(): lax.psum((grad_qkv_weight, grad_qv_bias, grad_proj_weight), 'dp')  72 us
    all_gather x1, waiting for transfers between devices, on_device(): grad_branch_full = lax.all_gather(grad_branch, 'tensor', axis=0, tiled=True)  70.3 us
    all_gather x1, waiting for transfers between devices, on_device(): lax.all_gather(normed2.astype(jnp.bfloat16), 'tensor', axis=0, tiled=True)  68.8 us
    reduce_scatter x1, waiting for transfers between devices, on_device(): lax.psum_scatter(jnp.dot(active, fc2_weight, preferred_element_type=jnp.f...  65.7 us
  transfers between devices with their start and end apart: 9, of which 9 were waited for; matrix products, arithmetic and copies ran while one was open for 4% of the time, Pallas kernels for 0%

commit v1 on v0

--- a/solution.py
+++ b/solution.py
@@ -230,17 +230,20 @@
         grad_fc2_bias,
         grad_scale_two,
     ) = lax.psum(
-        (
-            grad_ln1_gain,
-            grad_ln1_bias,
-            grad_proj_bias,
-            grad_scale_one,
-            grad_ln2_gain,
-            grad_ln2_bias,
-            grad_fc2_bias,
-            grad_scale_two,
+        lax.psum(
+            (
+                grad_ln1_gain,
+                grad_ln1_bias,
+                grad_proj_bias,
+                grad_scale_one,
+                grad_ln2_gain,
+                grad_ln2_bias,
+                grad_fc2_bias,
+                grad_scale_two,
+            ),
+            "dp",
         ),
-        ("dp", "tensor"),
+        "tensor",
     )
     return (
         block_out,

time: 1210 us -> 1210 us (level)
  blocking collectives: 57.3 us -> 45.1 us
    psum x1, blocking collectives: 42.2 us -> 26 us  [on_device(): lax.psum((grad_ln1_gain, grad_ln1_bias, grad_proj_bias, grad_scale_one, g...]
    reduce_scatter x1, waiting for transfers between devices: 30.6 us -> 45.8 us  [on_device(): lax.psum_scatter(jnp.einsum('tse,tde->sd', stacked, qkv_weight, preferred...]
where the time goes in v1:
time: 1210 us; the launch traced here: 1200 us
  waiting for transfers between devices  686 us (57%)
  matrix products  286 us (24%)
  other arithmetic  126 us (10%)
  blocking collectives  45.1 us (4%)
  local copies, waits for them, and re-layouts  27.9 us (2%)
  loops' own time  16.4 us (1%)
  between operations  14.6 us (1%)
    reduce_scatter x1, waiting for transfers between devices, on_device(): lax.psum_scatter(jnp.dot(attended, proj_weight, preferred_element_type=jn...  122 us
    reduce_scatter x1, waiting for transfers between devices, on_device(): lax.psum_scatter(jnp.einsum('sf,df->sd', grad_pre, fc1_weight, preferred_...  110 us
    dot_general x8, matrix products, scores_of(): jnp.einsum('qhd,khd->hqk', query_block, key_rows, preferred_element_type=...  75.1 us
    all_gather x1, waiting for transfers between devices, on_device(): lax.all_gather(normed1.astype(jnp.bfloat16), 'tensor', axis=0, tiled=True)  72.5 us
    all_gather x1, waiting for transfers between devices, on_device(): grad_branch_full = lax.all_gather(grad_branch, 'tensor', axis=0, tiled=True)  70.3 us
    psum x1, waiting for transfers between devices, on_device(): lax.psum((grad_qkv_weight, grad_qv_bias, grad_proj_weight), 'dp')  68.9 us
    all_gather x1, waiting for transfers between devices, on_device(): lax.all_gather(normed2.astype(jnp.bfloat16), 'tensor', axis=0, tiled=True)  68.8 us
    reduce_scatter x1, waiting for transfers between devices, on_device(): lax.psum_scatter(jnp.dot(active, fc2_weight, preferred_element_type=jnp.f...  65.7 us
  transfers between devices with their start and end apart: 9, of which 9 were waited for; matrix products, arithmetic and copies ran while one was open for 4% of the time, Pallas kernels for 0%

profile of v1, /device:TPU:0, one launch (start us, length us, event | category | flops | bytes accessed | tf_op | source)
XLA Modules:
  0.0 1202.7 jit_solution(1884693945269005314)
XLA Ops:
  13.2 72.5 %all-gather.5.cloned.1.call-done = bf16[2304,768]{1,0:T(8,128)(2,1)} async-done(((bf16[576,768]{1,0:T(8,128)(2,1)}), bf16[2304,768]{1,0:T(8,128)(2,1)}) %all-gather.5.cloned.1.call-update) | async-done | bytes 3538960 | tf_op jit(solution)/shard_map/all_gather | solution.py:61
  91.9 132.6 %while.27 = (s32[]{:T(128)}, bf16[4,576,3,64]{1,3,2,0:T(8,128)(2,1)}, f32[4,3,576]{2,1,0:T(4,128)S(1)}, s32[4]{0:T(128)S(1)}, s32[2304]{0:T(1024)S(1)}, /*index=...) while((s32[]{:T(128)}, ...), condition=%wide.region_5.6_spmd, body=%wide.region_2.5_spmd.sunk | while | flops 1068427584 | bytes 55445184 | solution.py:92
  103.9 10.0 fusion.122
  113.9 11.2 fusion.123
  147.0 11.2 fusion.123
  170.1 10.0 fusion.122
  180.1 11.2 fusion.123
  213.1 11.2 fusion.123
  233.7 122.2 %reduce-scatter.5.cloned.1.call-done = f32[576,768]{1,0:T(8,128)} async-done(((f32[2304,768]{1,0:T(8,128)}), f32[576,768]{1,0:T(8,128)}) %reduce-scatter.5.cloned.1.call-update) | async-done | bytes 1769488 | tf_op jit(solution)/shard_map/reduce_scatter | solution.py:95
  362.1 68.8 %all-gather.7.cloned.1.call-done = bf16[2304,768]{1,0:T(8,128)(2,1)} async-done(((bf16[576,768]{1,0:T(8,128)(2,1)}), bf16[2304,768]{1,0:T(8,128)(2,1)}) %all-gather.7.cloned.1.call-update) | async-done | bytes 3538960 | tf_op jit(solution)/shard_map/all_gather | solution.py:105
  439.2 62.4 %all-gather.9.cloned.1.call-done = bf16[2304,768]{1,0:T(8,128)(2,1)} async-done(((bf16[576,768]{1,0:T(8,128)(2,1)}), bf16[2304,768]{1,0:T(8,128)(2,1)}) %all-gather.9.cloned.1.call-update) | async-done | bytes 3538960 | tf_op jit(solution)/shard_map/all_gather | solution.py:122
  501.6 22.6 %convert_reduce_fusion = (f32[768]{0:T(1024)}, bf16[2304,768]{1,0:T(8,128)(2,1)S(1)}, f32[2304,768]{1,0:T(8,128)}) fusion(f32[2304,768]{1,0:T(8,128)} %fusion.68, f32[768]{0:T(1024)S(1)} %copy-done.47, bf16[2304,768]{1,0:T(8,128)(2,1)} %all-gather.9.cloned.1.call-done, bf16[768,768]{1,0:T(8,128)(2,1)S(1)} %copy-done), kind=kOutput, calls=%fused_computation.43 | convolution fusion | flops 2850618624 | bytes 22419456 | tf_op jit(solution)/shard_map/sd,fd->sf/dot_general | solution.py:126
  543.8 109.6 %reduce-scatter.9.cloned.1.call-done = f32[576,768]{1,0:T(8,128)} async-done(((f32[2304,768]{1,0:T(8,128)}), f32[576,768]{1,0:T(8,128)}) %reduce-scatter.9.cloned.1.call-update) | async-done | bytes 1769488 | tf_op jit(solution)/shard_map/reduce_scatter | solution.py:135
  656.7 65.7 %reduce-scatter.7.cloned.1.call-done = bf16[576,768]{1,0:T(8,128)(2,1)} async-done(((bf16[2304,768]{1,0:T(8,128)(2,1)}), bf16[576,768]{1,0:T(8,128)(2,1)}) %reduce-scatter.7.cloned.1.call-update) | async-done | bytes 884752 | tf_op jit(solution)/shard_map/reduce_scatter | solution.py:109
  730.1 70.3 %all-gather.11.cloned.1.call-done = bf16[2304,768]{1,0:T(8,128)(2,1)} async-done(((bf16[576,768]{1,0:T(8,128)(2,1)}), bf16[2304,768]{1,0:T(8,128)(2,1)}) %all-gather.11.cloned.1.call-update) | async-done | bytes 3538960 | tf_op jit(solution)/shard_map/all_gather | solution.py:148
  803.8 188.0 %while.28 = (s32[]{:T(128)}, f32[2304,3,64]{0,2,1:T(8,128)}, f32[2304,3,64]{0,2,1:T(8,128)}, bf16[4,576,3,64]{1,3,2,0:T(8,128)(2,1)}, s32[4]{0:T(128)S(1)}, /*in...) while((s32[]{:T(128)}, f32[2304,3,64]{0,2,1:T(8,128)}, ...), condition=%wide.region_15.16_spmd.clone, body=%wide.region_13.15_spmd.clone.sunk | while | flops 2587519232 | bytes 182914960 | solution.py:188
  816.5 10.3 multiply_reduce_fusion.7
  862.5 10.3 multiply_reduce_fusion.7
  909.8 10.3 multiply_reduce_fusion.7
  957.0 10.4 multiply_reduce_fusion.7
  1024.4 45.8 %reduce-scatter.11.cloned.1.call-done = bf16[576,768]{1,0:T(8,128)(2,1)} async-done(((bf16[2304,768]{1,0:T(8,128)(2,1)}), bf16[576,768]{1,0:T(8,128)(2,1)}) %reduce-scatter.11.cloned.1.call-update) | async-done | bytes 884752 | tf_op jit(solution)/shard_map/reduce_scatter | solution.py:205
  1072.4 26.0 %all-reduce = (f32[768]{0:T(1024)S(1)}, f32[768]{0:T(1024)S(1)}, f32[2,192]{1,0:T(2,128)}, f32[768]{0:T(1024)S(1)}, f32[768]{0:T(1024)S(1)}, /*index=5*/f32[768]...) all-reduce(f32[768]{0:T(1024)S(1)} %get-tuple-element.174, ...), channel_id=1, replica_groups=mesh['dp'=8,'tensor'=4] {'dp'}, use_global_device_ids=true, to_apply=%region_20.21 | all-reduce | flops 7296 | bytes 58368 | tf_op jit(solution)/shard_map/psum | solution.py:233
  1098.4 19.1 %all-reduce.2 = (f32[768]{0:T(1024)}, f32[768]{0:T(1024)}, f32[768]{0:T(1024)}, f32[768]{0:T(1024)}, f32[768]{0:T(1024)}, /*index=5*/f32[768]{0:T(1024)}, f32[768]{0:T(1024)}, f32[768]{0:T(1024)}) all-reduce(f32[768]{0:T(1024)S(1)} %get-tuple-element.224, ...), channel_id=1, replica_groups=mesh['dp'=8,'tensor'=4] {'tensor'}, use_global_device_ids=true, to_apply=%region_21.22 | all-reduce | flops 6144 | bytes 49152 | tf_op jit(solution)/shard_map/psum | solution.py:232
  1120.5 68.9 %all-reduce.5.cloned.1.call-done = (f32[3,768,192]{1,2,0:T(8,128)}, f32[192,768]{1,0:T(8,128)}, f32[768,768]{1,0:T(8,128)}, f32[768,768]{1,0:T(8,128)}) async-done(((f32[3,768,192]{1,2,0:T(8,128)}, f32[192,768]{1,0:T(8,128)}, f32[768,768]{1,0:T(8,128)}, f32[768,768]{1,0:T(8,128)}), (f32[3,768,192]{1,2,0:T(8,128)}, f32[192,768]{1,0:T(8,128)}, f32[768,768]{1,0:T(8,128)}, ...) | async-done | bytes 7077904 | tf_op jit(solution)/shard_map/psum | solution.py:220
  (291 shorter events, 311.7 us)
Async XLA Ops:
  7.2 494.4 %copy-start = (bf16[768,768]{1,0:T(8,128)(2,1)S(1)}, bf16[768,768]{1,0:T(8,128)(2,1)}, u32[]{:S(2)}) copy-start(bf16[768,768]{1,0:T(8,128)(2,1)} %param.34) | copy-start | bytes 3538948
  7.2 78.5 %copy-start.54 = (bf16[3,768,192]{1,2,0:T(8,128)(2,1)S(1)}, bf16[3,768,192]{1,2,0:T(8,128)(2,1)}, u32[]{:S(2)}) copy-start(bf16[3,768,192]{1,2,0:T(8,128)(2,1)} %param.25) | copy-start | bytes 2654212
  7.2 78.5 %all-gather.5.cloned.1.call-start = ((), (), s32[]{:S(2)}) async-start(), calls=%async_computation.4 | async-start | bytes 4423680 | tf_op jit(solution)/shard_map/all_gather | solution.py:61
  8.8 81.2 %copy-start.31 = (f32[576]{0:T(1024)}, f32[576]{0:T(1024)S(1)}, u32[]{:S(2)}) copy-start(f32[576]{0:T(1024)S(1)} %broadcast_multiply_fusion.5) | copy-start | bytes 6916
  10.4 79.6 %copy-start.33 = (f32[576]{0:T(1024)}, f32[576]{0:T(1024)S(1)}, u32[]{:S(2)}) copy-start(f32[576]{0:T(1024)S(1)} %add_rsqrt_fusion.1) | copy-start | bytes 6916
  12.9 343.0 %reduce-scatter.5.cloned.1.call-start = ((), (), s32[]{:S(2)}) async-start(), calls=%async_computation.5 | async-start | bytes 8847360 | tf_op jit(solution)/shard_map/reduce_scatter | solution.py:95
  233.6 122.3 %copy-start.6 = (bf16[576,768]{1,0:T(8,128)(2,1)S(1)}, bf16[576,768]{1,0:T(8,128)(2,1)}, u32[]{:S(2)}) copy-start(bf16[576,768]{1,0:T(8,128)(2,1)} %param.21) | copy-start | bytes 2654212
  233.6 122.3 %copy-start.37 = (f32[768]{0:T(1024)S(1)}, f32[768]{0:T(1024)}, u32[]{:S(2)}) copy-start(f32[768]{0:T(1024)} %param.28) | copy-start | bytes 9220
  233.6 122.3 %copy-start.39 = (f32[768]{0:T(1024)S(1)}, f32[768]{0:T(1024)}, u32[]{:S(2)}) copy-start(f32[768]{0:T(1024)} %param.29) | copy-start | bytes 9220
  233.7 125.3 %copy-start.36 = (f32[768]{0:T(1024)S(1)}, f32[768]{0:T(1024)}, u32[]{:S(2)}) copy-start(f32[768]{0:T(1024)} %param.30) | copy-start | bytes 9220
  233.7 125.3 %copy-start.46 = (f32[768]{0:T(1024)S(1)}, f32[768]{0:T(1024)}, u32[]{:S(2)}) copy-start(f32[768]{0:T(1024)} %param.31) | copy-start | bytes 9220
  233.7 197.3 %all-gather.7.cloned.1.call-start = ((), (), s32[]{:S(2)}) async-start(), calls=%async_computation.6 | async-start | bytes 4423680 | tf_op jit(solution)/shard_map/all_gather | solution.py:105
  360.3 141.3 %all-gather.9.cloned.1.call-start = ((), (), s32[]{:S(2)}) async-start(), calls=%async_computation.8 | async-start | bytes 4423680 | tf_op jit(solution)/shard_map/all_gather | solution.py:122
  362.1 139.5 %copy-start.47 = (f32[768]{0:T(1024)S(1)}, f32[768]{0:T(1024)}, u32[]{:S(2)}) copy-start(f32[768]{0:T(1024)} %param.33) | copy-start | bytes 9220
  362.1 291.2 %reduce-scatter.9.cloned.1.call-start = ((), (), s32[]{:S(2)}) async-start(), calls=%async_computation.9 | async-start | bytes 8847360 | tf_op jit(solution)/shard_map/reduce_scatter | solution.py:135
  531.1 191.3 %reduce-scatter.7.cloned.1.call-start = ((), (), s32[]{:S(2)}) async-start(), calls=%async_computation.7 | async-start | bytes 4423680 | tf_op jit(solution)/shard_map/reduce_scatter | solution.py:109
  543.7 178.7 %copy-start.48 = (f32[768]{0:T(1024)S(1)}, f32[768]{0:T(1024)}, u32[]{:S(2)}) copy-start(f32[768]{0:T(1024)} %param.35) | copy-start | bytes 9220
  543.7 256.8 %all-gather.11.cloned.1.call-start = ((), (), s32[]{:S(2)}) async-start(), calls=%async_computation.10 | async-start | bytes 4423680 | tf_op jit(solution)/shard_map/all_gather | solution.py:148
  730.0 73.8 %copy-start.8 = (bf16[2304,3,64]{0,2,1:T(8,128)(2,1)S(1)}, bf16[2304,3,64]{0,2,1:T(8,128)(2,1)}, u32[]{:S(2)}) copy-start(bf16[2304,3,64]{0,2,1:T(8,128)(2,1)} %get-tuple-element.521) | copy-start | bytes 2654212
  730.1 340.1 %reduce-scatter.11.cloned.1.call-start = ((), (), s32[]{:S(2)}) async-start(), calls=%async_computation.11 | async-start | bytes 4423680 | tf_op jit(solution)/shard_map/reduce_scatter | solution.py:205
  1005.1 184.2 %all-reduce.5.cloned.1.call-start = ((), (), s32[]{:S(2)}) async-start(), calls=%async_computation.12 | async-start | bytes 14155776 | tf_op jit(solution)/shard_map/psum | solution.py:220
  1022.5 49.8 %copy-start.40 = (f32[768]{0:T(1024)S(1)}, f32[768]{0:T(1024)}, u32[]{:S(2)}) copy-start(f32[768]{0:T(1024)} %get-tuple-element.246) | copy-start | bytes 9220
  1022.5 49.8 %copy-start.41 = (f32[768]{0:T(1024)S(1)}, f32[768]{0:T(1024)}, u32[]{:S(2)}) copy-start(f32[768]{0:T(1024)} %get-tuple-element.251) | copy-start | bytes 9220
  1022.6 94.9 %copy-start.11 = (f32[576,768]{1,0:T(8,128)S(1)}, f32[576,768]{1,0:T(8,128)}, u32[]{:S(2)}) copy-start(f32[576,768]{1,0:T(8,128)} %copy-done.10) | copy-start | bytes 5308420
  (59 other events, 679.3 us)
Sparse Core Ops, SparseCore 0:
  13.0 72.6 all-gather.4
  233.8 122.0 reduce-scatter.4
  360.4 70.5 all-gather.6
  433.0 68.5 all-gather.8
  531.2 122.0 reduce-scatter.8
  655.5 66.8 reduce-scatter.6
  730.2 70.2 all-gather.10
  1005.2 64.9 reduce-scatter.10
  1075.0 114.2 all-reduce.4
